TPU v7x, 32 devices: a whole 2x2x4 slice. The times are simulated.
32 devices in a mesh: ctx: 16 (over z, y, x), exp: 2 (over core).
Axes of the slice: x: 2, y: 2, z: 4, core: 2. Of those that a mesh axis runs over, the one named last changes fastest.
Arguments:
- attn_query: bfloat16 [2048, 4096], P('ctx', 'exp'), may hold values from -3 to 3
- attn_key: bfloat16 [2048, 4096], P('ctx', 'exp'), may hold values from -3 to 3
- attn_value: bfloat16 [2048, 4096], P('ctx', 'exp'), may hold values from -6 to 6
- log_decay: float32 [32, 2048], P('exp', 'ctx'), may hold values from -1 to 0
- cotangent: bfloat16 [2048, 4096], P('ctx', 'exp'), may hold values from -6 to 6
- expert_input: bfloat16 [2048, 4096], P('ctx', 'exp'), may hold values from -6 to 6
- router_gates: bfloat16 [2048, 4], P('ctx'), may hold values from 0.049804688 to 0.59765625
- expert_ids: int32 [2048, 4], P('ctx'), may hold values from 0 to 15, all different within a row; in each aligned block of 128 rows (0 to 127, 128 to 255, ...) at most 40 rows name the same one
- up_weights: bfloat16 [16, 4096, 1536], P('ctx', 'exp'), may hold values from -0.09375 to 0.09375
- down_weights: bfloat16 [16, 1536, 4096], P('ctx', None, 'exp'), may hold values from -0.15625 to 0.15625
Outputs:
- query_grad: bfloat16 [2048, 4096], P('ctx', 'exp')
- key_grad: bfloat16 [2048, 4096], P('ctx', 'exp')
- value_grad: bfloat16 [2048, 4096], P('ctx', 'exp')
- input_grad: bfloat16 [2048, 4096], P('ctx', 'exp')
- gate_grad: bfloat16 [2048, 4], P('ctx')
Inputs may be any that keep to these rules, and one draw needn't show every extreme that they name: `expert_ids`: each row names 4 different experts. Within the rows of one device (each aligned block of 128 rows) no expert is named more than 40 times, a bound that some block reaches.
All inputs are finite; a program needn't handle non-finite values.
Results may differ from a plain program's by a relative error of at most 0.025.
Values may be sent and summed in bfloat16 or wider, within the bound.
No kernel may reach another device: no remote copies, remote signals or barrier semaphores. Data moves between devices by JAX's collectives and lax.ppermute only.
A program may use at most 128 MiB of HBM per device.

v0:
```python
import jax
import jax.numpy as jnp
from jax import lax
from jax.sharding import PartitionSpec as P


def prefix(value, axis, join, neutral, backward):
    count = lax.axis_size(axis)
    place = lax.axis_index(axis)
    ahead = count - 1 - place if backward else place
    gathered = jax.tree.map(
        lambda a, kind: lax.all_gather(a.astype(kind), axis), value, (jnp.bfloat16, jnp.bfloat16)
    )
    state = jax.tree.map(lambda a, e: jnp.zeros_like(a) + jnp.asarray(e, a.dtype), value, neutral)

    def one(step, state):
        source = count - 1 - step if backward else step
        return join(
            state,
            jax.tree.map(
                lambda a, own: lax.dynamic_index_in_dim(a, source, 0, False).astype(own.dtype),
                gathered,
                value,
            ),
        )

    return lax.fori_loop(0, ahead, one, state)


def silu_slope(pre_act):
    sigmoid_val = jax.nn.sigmoid(pre_act)
    return sigmoid_val * (1.0 + pre_act * (1.0 - sigmoid_val))


def chain_step(earlier, later):
    return (earlier[0] + later[0], jnp.exp(later[0])[:, None, None] * earlier[1] + later[1])


def attention_part(attn_query, attn_key, attn_value, log_decay, cotangent):
    length, features = attn_query.shape
    head_count = log_decay.shape[0]
    head_size = features // head_count
    head_shape = (length, head_count, head_size)
    query_heads = attn_query.reshape(head_shape)
    key_head_rows = attn_key.reshape(head_shape)
    value_head_rows = attn_value.reshape(head_shape)
    cotangent_heads = cotangent.reshape(head_shape)
    cumul = jnp.cumsum(log_decay, axis=1)
    block_gain = cumul[:, -1]
    head_gain = jnp.exp(cumul).T[:, :, None]
    tail_gain = jnp.exp(block_gain[:, None] - cumul).T[:, :, None]
    scaled_key_rows = (tail_gain * key_head_rows).astype(jnp.bfloat16)
    scaled_query_rows = (head_gain * query_heads).astype(jnp.bfloat16)
    local_state = jnp.einsum(
        "qcb,qce->cbe", scaled_key_rows, value_head_rows, preferred_element_type=jnp.float32
    )
    local_adjoint = jnp.einsum(
        "iuo,iuf->uof", scaled_query_rows, cotangent_heads, preferred_element_type=jnp.float32
    )
    identity = (
        jnp.zeros((head_count,), jnp.float32),
        jnp.zeros((head_count, head_size, head_size), jnp.float32),
    )
    state_in = prefix((block_gain, local_state), "ctx", chain_step, identity, False)
    adjoint_in = prefix((block_gain, local_adjoint), "ctx", chain_step, identity, True)
    state_bfloat_copy = state_in[1].astype(jnp.bfloat16)
    adjoint_bfloat_copy = adjoint_in[1].astype(jnp.bfloat16)
    row_index = lax.broadcasted_iota(jnp.int32, (length, length), 0)
    col_index = lax.broadcasted_iota(jnp.int32, (length, length), 1)
    causal = (row_index >= col_index)[None, :, :]
    spread = cumul[:, :, None] - cumul[:, None, :]
    decay_mask = jnp.where(causal, jnp.exp(jnp.where(causal, spread, 0.0)), 0.0)
    cross_terms = jnp.einsum(
        "thv,shv->hts", cotangent_heads, value_head_rows, preferred_element_type=jnp.float32
    )
    scores = jnp.einsum(
        "thk,shk->hts", query_heads, key_head_rows, preferred_element_type=jnp.float32
    )
    cross_weights = (cross_terms * decay_mask).astype(jnp.bfloat16)
    score_weights = (scores * decay_mask).astype(jnp.bfloat16)
    query_part = jnp.einsum(
        "hts,shk->thk", cross_weights, key_head_rows, preferred_element_type=jnp.float32
    )
    query_part = query_part + head_gain * jnp.einsum(
        "gmi,mli->gml", cotangent_heads, state_bfloat_copy, preferred_element_type=jnp.float32
    )
    key_part = jnp.einsum(
        "hts,thk->shk", cross_weights, query_heads, preferred_element_type=jnp.float32
    )
    key_part = key_part + tail_gain * jnp.einsum(
        "ecf,cpf->ecp", value_head_rows, adjoint_bfloat_copy, preferred_element_type=jnp.float32
    )
    value_part = jnp.einsum(
        "hts,thv->shv", score_weights, cotangent_heads, preferred_element_type=jnp.float32
    )
    value_part = value_part + tail_gain * jnp.einsum(
        "owr,wru->owu", key_head_rows, adjoint_bfloat_copy, preferred_element_type=jnp.float32
    )
    scale = 1.0 / head_size
    query_grad = (query_part * scale).reshape(length, features).astype(jnp.bfloat16)
    key_grad = (key_part * scale).reshape(length, features).astype(jnp.bfloat16)
    value_grad = (value_part * scale).reshape(length, features).astype(jnp.bfloat16)
    return (query_grad, key_grad, value_grad)


def expert_part(cotangent, expert_input, router_gates, expert_ids, up_weights, down_weights):
    tokens, feature_share = expert_input.shape
    top_count = expert_ids.shape[1]
    experts = lax.axis_size("ctx")
    capacity = 5 * tokens * top_count // (4 * experts)
    flat_ids = expert_ids.reshape(-1)
    onehot = (flat_ids[:, None] == jnp.arange(experts, dtype=jnp.int32)[None, :]).astype(jnp.int32)
    before = jnp.cumsum(onehot, axis=0) - onehot
    slot_index = jnp.sum(before * onehot, axis=1)
    target = (flat_ids * capacity + slot_index).reshape(tokens, top_count)
    placed = target[None, :, :] == jnp.arange(experts * capacity, dtype=jnp.int32)[:, None, None]
    placed_float = placed.astype(jnp.float32)
    dispatch_rows = jnp.sum(placed_float, axis=2).astype(jnp.bfloat16)
    buffer_in = jnp.dot(dispatch_rows, expert_input, preferred_element_type=jnp.float32).astype(
        jnp.bfloat16
    )
    buffer_cot = jnp.dot(dispatch_rows, cotangent, preferred_element_type=jnp.float32).astype(
        jnp.bfloat16
    )
    buffer_gate = jnp.einsum("jtk,tk->j", placed_float, router_gates.astype(jnp.float32)).astype(
        jnp.bfloat16
    )
    buffer_in = buffer_in.reshape(experts, capacity, feature_share)
    buffer_cot = buffer_cot.reshape(experts, capacity, feature_share)
    buffer_gate = buffer_gate.reshape(experts, capacity)
    up_local = up_weights[0]
    down_local = down_weights[0]
    inputs = lax.all_to_all(buffer_in, "ctx", split_axis=0, concat_axis=0, tiled=True)
    cot_rows = lax.all_to_all(buffer_cot, "ctx", split_axis=0, concat_axis=0, tiled=True)
    gate_rows = lax.all_to_all(buffer_gate, "ctx", split_axis=0, concat_axis=0, tiled=True)
    sources, item_count, share_width = inputs.shape
    flat_in = inputs.reshape(sources * item_count, share_width)
    flat_cot = cot_rows.reshape(sources * item_count, share_width)
    gate_col = gate_rows.reshape(-1).astype(jnp.float32)
    part_pre = jnp.dot(flat_in, up_local, preferred_element_type=jnp.float32)
    part_back = lax.dot_general(
        flat_cot, down_local, (((1,), (1,)), ((), ())), preferred_element_type=jnp.float32
    )
    pre_act = lax.psum(part_pre.astype(jnp.bfloat16), "exp").astype(jnp.float32)
    back_rows = lax.psum(part_back.astype(jnp.bfloat16), "exp").astype(jnp.float32)
    gate_back = jnp.sum(back_rows * jax.nn.silu(pre_act), axis=1)
    slope_rows = (gate_col[:, None] * back_rows * silu_slope(pre_act)).astype(jnp.bfloat16)
    rows_grad = lax.dot_general(
        slope_rows, up_local, (((1,), (1,)), ((), ())), preferred_element_type=jnp.float32
    )
    rows_grad = rows_grad.astype(jnp.bfloat16).reshape(sources, item_count, share_width)
    gate_back = gate_back.astype(jnp.bfloat16).reshape(sources, item_count)
    grad_buffer = lax.all_to_all(rows_grad, "ctx", split_axis=0, concat_axis=0, tiled=True)
    gate_buffer = lax.all_to_all(gate_back, "ctx", split_axis=0, concat_axis=0, tiled=True)
    grad_flat = grad_buffer.reshape(experts * capacity, feature_share)
    input_grad = lax.dot_general(
        dispatch_rows, grad_flat, (((0,), (0,)), ((), ())), preferred_element_type=jnp.float32
    )
    gate_grad = jnp.einsum("jtk,j->tk", placed_float, gate_buffer.reshape(-1).astype(jnp.float32))
    return (input_grad.astype(jnp.bfloat16), gate_grad.astype(jnp.bfloat16))


def body(
    attn_query,
    attn_key,
    attn_value,
    log_decay,
    cotangent,
    expert_input,
    router_gates,
    expert_ids,
    up_weights,
    down_weights,
):
    query_grad, key_grad, value_grad = attention_part(
        attn_query, attn_key, attn_value, log_decay, cotangent
    )
    input_grad, gate_grad = expert_part(
        cotangent, expert_input, router_gates, expert_ids, up_weights, down_weights
    )
    return (query_grad, key_grad, value_grad, input_grad, gate_grad)


def solution(mesh):
    return jax.shard_map(
        body,
        mesh=mesh,
        in_specs=(
            P("ctx", "exp"),
            P("ctx", "exp"),
            P("ctx", "exp"),
            P("exp", "ctx"),
            P("ctx", "exp"),
            P("ctx", "exp"),
            P("ctx", None),
            P("ctx", None),
            P("ctx", "exp", None),
            P("ctx", None, "exp"),
        ),
        out_specs=(
            P("ctx", "exp"),
            P("ctx", "exp"),
            P("ctx", "exp"),
            P("ctx", "exp"),
            P("ctx", None),
        ),
        check_vma=False,
    )
```

profile of v0, /device:TPU:31, one launch (start us, length us, event | category | flops | bytes accessed | tf_op | source)
XLA Modules:
  0.0 465.7 jit_solution(6112903337878251845)
XLA Ops:
  11.6 3.4 convolution_convert_fusion.1
  15.0 6.4 %all-to-all-start.1 = ((bf16[16,40,2048]{2,1,0:T(8,128)(2,1)}), bf16[16,40,2048]{2,1,0:T(8,128)(2,1)S(1)}, u32[]{:S(2)}, u32[]{:S(2)}) async-start(bf16[16,40,2048]{2,1,0:T(8,128)(2,1)} %bitcast.22), calls=%async_computation.1 | async-start | bytes 5242880 | tf_op jit(solution)/shard_map/all_to_all | solution.py:134
  21.4 2.4 convolution_convert_fusion
  23.7 54.2 %all-to-all-done.1 = bf16[16,40,2048]{2,1,0:T(8,128)(2,1)S(1)} async-done(((bf16[16,40,2048]{2,1,0:T(8,128)(2,1)}), bf16[16,40,2048]{2,1,0:T(8,128)(2,1)S(1)}, u32[]{:S(2)}, u32[]{:S(2)}) %all-to-all-start.1) | async-done | bytes 2621472 | tf_op jit(solution)/shard_map/all_to_all | solution.py:134
  77.9 7.0 %all-to-all-start.2 = ((bf16[16,40,2048]{2,1,0:T(8,128)(2,1)}), bf16[16,40,2048]{2,1,0:T(8,128)(2,1)}, u32[]{:S(2)}, u32[]{:S(2)}) async-start(bf16[16,40,2048]{2,1,0:T(8,128)(2,1)} %bitcast.25), calls=%async_computation.2 | async-start | bytes 5242880 | tf_op jit(solution)/shard_map/all_to_all | solution.py:133
  85.0 8.3 %fusion.14 = bf16[640,1536]{1,0:T(8,128)(2,1)} fusion(bf16[640,2048]{1,0:T(8,128)(2,1)S(1)} %bitcast.160, bf16[1,1536,2048]{2,1,0:T(8,128)(2,1)} %param.23), kind=kOutput, calls=%fused_computation.23 | convolution fusion | flops 4027514880 | bytes 10878976 | tf_op jit(solution)/shard_map/dot_general | solution.py:141
  93.2 47.2 %all-to-all-done.2 = bf16[16,40,2048]{2,1,0:T(8,128)(2,1)} async-done(((bf16[16,40,2048]{2,1,0:T(8,128)(2,1)}), bf16[16,40,2048]{2,1,0:T(8,128)(2,1)}, u32[]{:S(2)}, u32[]{:S(2)}) %all-to-all-start.2) | async-done | bytes 2621472 | tf_op jit(solution)/shard_map/all_to_all | solution.py:133
  140.4 9.1 %fusion.17 = bf16[640,1536]{1,0:T(8,128)(2,1)} fusion(bf16[640,2048]{1,0:T(8,128)(2,1)} %bitcast.26, bf16[1,2048,1536]{2,1,0:T(8,128)(2,1)} %param.22), kind=kOutput, calls=%fused_computation.24 | convolution fusion | flops 4027514880 | bytes 10878976 | tf_op jit(solution)/shard_map/dot_general | solution.py:140
  155.0 9.3 %all_to_all.31 = bf16[16,1,40]{2,1,0:T(2,128)(2,1)S(1)} all-to-all(bf16[16,1,40]{2,1,0:T(2,128)(2,1)S(1)} %all_to_all.25), channel_id=1, replica_groups=mesh['ctx'=16,'exp'=2] {'ctx'}, dimensions={0} | all-to-all | bytes 2560 | tf_op jit(solution)/shard_map/all_to_all | solution.py:135
  164.4 14.2 %all-reduce.4.cloned.1.call-done = (bf16[640,1536]{1,0:T(8,128)(2,1)}, bf16[640,1536]{1,0:T(8,128)(2,1)}) async-done(((bf16[640,1536]{1,0:T(8,128)(2,1)}, bf16[640,1536]{1,0:T(8,128)(2,1)}), (bf16[640,1536]{1,0:T(8,128)(2,1)}, bf16[640,1536]{1,0:T(8,128)(2,1)})) %all-reduce.4.cloned.1.call-update) | async-done | bytes 3932176 | tf_op jit(solution)/shard_map/psum | solution.py:145
  178.6 3.4 fusion.8
  182.7 6.4 %all-to-all-start.4 = ((bf16[16,1,40]{2,1,0:T(2,128)(2,1)}), bf16[16,1,40]{2,1,0:T(2,128)(2,1)S(1)}, u32[]{:S(2)}, u32[]{:S(2)}) async-start(bf16[16,1,40]{2,1,0:T(2,128)(2,1)} %convert_element_type.212), calls=%async_computation.4 | async-start | bytes 16384 | tf_op jit(solution)/shard_map/all_to_all | solution.py:154
  189.1 10.5 %fusion.20 = bf16[640,2048]{1,0:T(8,128)(2,1)} fusion(bf16[1,2048,1536]{2,1,0:T(8,128)(2,1)} %param.22, bf16[640,1536]{1,0:T(8,128)(2,1)} %get-tuple-element.180, bf16[640,1536]{1,0:T(8,128)(2,1)} %get-tuple-element.181, f32[640]{0:T(1024)S(1)} %reshape.161), kind=kOutput, calls=%fused_computation.25 | convolution fusion | flops 4039639040 | bytes 12847616 | tf_op jit(solution)/shard_map/dot_general | solution.py:148
  199.6 6.4 %all-to-all-start.3 = ((bf16[16,40,2048]{2,1,0:T(8,128)(2,1)}), bf16[16,40,2048]{2,1,0:T(8,128)(2,1)S(1)}, u32[]{:S(2)}, u32[]{:S(2)}) async-start(bf16[16,40,2048]{2,1,0:T(8,128)(2,1)} %bitcast.159), calls=%async_computation.3 | async-start | bytes 5242880 | tf_op jit(solution)/shard_map/all_to_all | solution.py:153
  207.6 116.0 %all-reduce = bf16[256]{0:T(256)(128)(2,1)S(1)} all-reduce(bf16[256]{0:T(256)(128)(2,1)S(1)} %dynamic-update-slice), channel_id=2, replica_groups=mesh['ctx'=16,'exp'=2] {'ctx'}, use_global_device_ids=true, to_apply=%add | all-reduce | flops 256 | bytes 1024
  323.7 1.8 fusion.39
  326.3 1.5 convolution_bitcast_fusion.5
  331.3 1.6 fusion.31
  334.2 93.8 %all-gather.6.cloned.1.call-done = bf16[256,128,128]{2,1,0:T(8,128)(2,1)} async-done(((bf16[16,128,128]{2,1,0:T(8,128)(2,1)}), bf16[256,128,128]{2,1,0:T(8,128)(2,1)}) %all-gather.6.cloned.1.call-update) | async-done | bytes 8388624 | tf_op jit(solution)/shard_map/all_gather | solution.py:12
  428.0 20.2 %while.26 = (s32[]{:T(128)}, f32[16,128,128]{2,1,0:T(8,128)S(1)}, s32[]{:T(128)}, bf16[16,16]{1,0:T(8,128)(2,1)S(1)}, bf16[16,16,128,128]{3,2,1,0:T(8,128)(2,1)}, /*index=5*/s32[]{:T(128)}, s32[]{:T(128)}, s32[]{:T(128)}) while((s32[]{:T(128)}, f32[16,128,128]{2,1,0:T(8,128)S(1)}, s32[]{:T(128)}, bf16[16,16]{1,0:T(8,128)(2,1)S(1)}, ...), condition=%wide.region_2.3_spmd, body=%wide.region_1.2_spmd.sunk | while | flops 786453 | bytes 2621735 | solution.py:27
  448.2 2.4 fusion.40
  450.6 2.1 copy.115
  452.7 1.5 fusion.37
  455.3 1.9 fusion.38
  (114 shorter events, 38.2 us)
Async XLA Ops:
  8.0 13.4 %copy-start = (bf16[128,2048]{1,0:T(8,128)(2,1)S(1)}, bf16[128,2048]{1,0:T(8,128)(2,1)}, u32[]{:S(2)}) copy-start(bf16[128,2048]{1,0:T(8,128)(2,1)} %param.19) | copy-start | bytes 1572868
  15.0 62.9 %all-to-all-start.1 = ((bf16[16,40,2048]{2,1,0:T(8,128)(2,1)}), bf16[16,40,2048]{2,1,0:T(8,128)(2,1)S(1)}, u32[]{:S(2)}, u32[]{:S(2)}) async-start(bf16[16,40,2048]{2,1,0:T(8,128)(2,1)} %bitcast.22), calls=%async_computation.1 | async-start | bytes 5242880 | tf_op jit(solution)/shard_map/all_to_all | solution.py:134
  77.9 62.5 %all-to-all-start.2 = ((bf16[16,40,2048]{2,1,0:T(8,128)(2,1)}), bf16[16,40,2048]{2,1,0:T(8,128)(2,1)}, u32[]{:S(2)}, u32[]{:S(2)}) async-start(bf16[16,40,2048]{2,1,0:T(8,128)(2,1)} %bitcast.25), calls=%async_computation.2 | async-start | bytes 5242880 | tf_op jit(solution)/shard_map/all_to_all | solution.py:133
  84.9 93.7 %all-reduce.4.cloned.1.call-start = ((), (), s32[]{:S(2)}) async-start(), calls=%async_computation.7 | async-start | bytes 7864320 | tf_op jit(solution)/shard_map/psum | solution.py:145
  149.5 1.0 copy-start.8
  149.5 1.3 copy-start.11
  149.5 1.6 copy-start.13
  149.6 3.5 copy-start.12
  149.6 3.8 copy-start.6
  149.6 4.9 %copy-start.14 = (bf16[128,4]{0,1:T(4,128)(2,1)S(1)}, bf16[128,4]{0,1:T(4,128)(2,1)}, u32[]{:S(2)}) copy-start(bf16[128,4]{0,1:T(4,128)(2,1)} %param.20) | copy-start | bytes 3076
  149.6 180.5 %all-gather.8.cloned.1.call-start = ((), (), s32[]{:S(2)}) async-start(), calls=%async_computation.6 | async-start | bytes 8912896 | tf_op jit(solution)/shard_map/all_gather | solution.py:12
  150.9 48.7 %copy-start.4 = (bf16[128,2048]{0,1:T(8,128)(2,1)}, bf16[128,2048]{0,1:T(8,128)(2,1)S(1)}, u32[]{:S(2)}) copy-start(bf16[128,2048]{0,1:T(8,128)(2,1)S(1)} %copy.124) | copy-start | bytes 1572868
  151.2 30.9 %copy-start.2 = (bf16[128,2048]{0,1:T(8,128)(2,1)}, bf16[128,2048]{0,1:T(8,128)(2,1)S(1)}, u32[]{:S(2)}) copy-start(bf16[128,2048]{0,1:T(8,128)(2,1)S(1)} %copy.101) | copy-start | bytes 1572868
  153.0 274.9 %all-gather.6.cloned.1.call-start = ((), (), s32[]{:S(2)}) async-start(), calls=%async_computation.5 | async-start | bytes 8912896 | tf_op jit(solution)/shard_map/all_gather | solution.py:12
  182.7 16.9 %all-to-all-start.4 = ((bf16[16,1,40]{2,1,0:T(2,128)(2,1)}), bf16[16,1,40]{2,1,0:T(2,128)(2,1)S(1)}, u32[]{:S(2)}, u32[]{:S(2)}) async-start(bf16[16,1,40]{2,1,0:T(2,128)(2,1)} %convert_element_type.212), calls=%async_computation.4 | async-start | bytes 16384 | tf_op jit(solution)/shard_map/all_to_all | solution.py:154
  199.6 6.4 %copy-start.15 = (u32[32]{0:T(128)S(1)}, u32[32]{0:T(128)}, u32[]{:S(2)}) copy-start(u32[32]{0:T(128)} %constant.80) | copy-start | bytes 388
  199.6 129.1 %all-to-all-start.3 = ((bf16[16,40,2048]{2,1,0:T(8,128)(2,1)}), bf16[16,40,2048]{2,1,0:T(8,128)(2,1)S(1)}, u32[]{:S(2)}, u32[]{:S(2)}) async-start(bf16[16,40,2048]{2,1,0:T(8,128)(2,1)} %bitcast.159), calls=%async_computation.3 | async-start | bytes 5242880 | tf_op jit(solution)/shard_map/all_to_all | solution.py:153
  325.5 0.8 copy-start.9
  330.2 1.0 copy-start.7
  428.0 20.2 %copy-start.5 = (bf16[128,2048]{0,1:T(8,128)(2,1)S(1)}, bf16[128,2048]{0,1:T(8,128)(2,1)}, u32[]{:S(2)}) copy-start(bf16[128,2048]{0,1:T(8,128)(2,1)} %copy-done.4) | copy-start | bytes 1572868
  448.2 4.5 copy-start.3
  448.2 4.5 copy-start.10
  450.6 7.6 %copy-start.1 = (bf16[128,2048]{1,0:T(8,128)(2,1)S(1)}, bf16[128,2048]{1,0:T(8,128)(2,1)}, u32[]{:S(2)}) copy-start(bf16[128,2048]{1,0:T(8,128)(2,1)} %param.19) | copy-start | bytes 1572868
Sparse Core Ops, SparseCore 0:
  149.7 28.8 all-reduce.3
Sparse Core Ops, SparseCore 1:
  153.4 160.4 all-gather.7
  317.1 110.8 all-gather.5
where the time goes:
time: 467 us; the launch traced here: 466 us
  waiting for transfers between devices  209 us (45%)
  blocking collectives  125 us (27%)
  matrix products  50 us (11%)
  other arithmetic  26.2 us (6%)
  starting transfers between devices  26.2 us (6%)
  between operations  16.4 us (4%)
  local copies, waits for them, and re-layouts  11.6 us (2%)
    unnamed x1, blocking collectives  116 us
    all_gather x2, waiting for transfers between devices, prefix(): lax.all_gather(a.astype(kind), axis)  93.8 us
    all_to_all x1, waiting for transfers between devices, expert_part(): lax.all_to_all(buffer_cot, 'ctx', split_axis=0, concat_axis=0, tiled=True)  54.2 us
    all_to_all x1, waiting for transfers between devices, expert_part(): lax.all_to_all(buffer_in, 'ctx', split_axis=0, concat_axis=0, tiled=True)  47.2 us
    add x15, other arithmetic, chain_step(): jnp.exp(later[0])[:, None, None] * earlier[1] + later[1]  19.5 us
    psum x1, waiting for transfers between devices, expert_part(): lax.psum(part_back.astype(jnp.bfloat16), 'exp').astype(jnp.float32)  14.2 us
    dot_general x1, matrix products, expert_part(): lax.dot_general(slope_rows, up_local, (((1,), (1,)), ((), ())), preferred...  10.5 us
  transfers between devices with their start and end apart: 7, of which 4 were waited for; matrix products, arithmetic and copies ran while one was open for 8% of the time, Pallas kernels for 0%

commit v1 on v0

--- a/solution.py
+++ b/solution.py
@@ -131,7 +131,19 @@
     up_local = up_weights[0]
     down_local = down_weights[0]
     inputs = lax.all_to_all(buffer_in, "ctx", split_axis=0, concat_axis=0, tiled=True)
-    cot_rows = lax.all_to_all(buffer_cot, "ctx", split_axis=0, concat_axis=0, tiled=True)
+    ways, here = (lax.axis_size("ctx"), lax.axis_index("ctx"))
+    width = buffer_cot.shape[0] // ways
+    dims = list(buffer_cot.shape)
+    dims[0] = width
+    height = dims[0]
+    dims[0] = height * ways
+    full = jnp.zeros(dims, buffer_cot.dtype)
+    for mask in range(ways):
+        part = lax.dynamic_slice_in_dim(buffer_cot, (here ^ mask) * width, width, axis=0)
+        if mask:
+            part = lax.ppermute(part, "ctx", [(d, d ^ mask) for d in range(ways)])
+        full = lax.dynamic_update_slice_in_dim(full, part, (here ^ mask) * height, axis=0)
+    cot_rows = full
     gate_rows = lax.all_to_all(buffer_gate, "ctx", split_axis=0, concat_axis=0, tiled=True)
     sources, item_count, share_width = inputs.shape
     flat_in = inputs.reshape(sources * item_count, share_width)

time: 467 us -> 468 us (level)
  waiting for transfers between devices: 209 us -> 174 us
  starting transfers between devices: 26.2 us -> 52.4 us
  blocking collectives: 125 us -> 140 us
  matrix products: 50 us -> 44.7 us
    ppermute x0 -> x15, waiting for transfers between devices: none -> 66.1 us  [expert_part(): part = lax.ppermute(part, 'ctx', [(d, d ^ mask) for d in range(ways)])]
    all_to_all x1 -> x0, waiting for transfers between devices: 54.2 us -> none  [expert_part(): lax.all_to_all(buffer_cot, 'ctx', split_axis=0, concat_axis=0, tiled=True)]
    all_to_all x1, waiting for transfers between devices: 47.2 us -> 0.01 us  [expert_part(): lax.all_to_all(buffer_in, 'ctx', split_axis=0, concat_axis=0, tiled=True)]
    ppermute x0 -> x15, starting transfers between devices: none -> 33 us  [expert_part(): part = lax.ppermute(part, 'ctx', [(d, d ^ mask) for d in range(ways)])]
    all_to_all x1, blocking collectives: 9.32 us -> 23.8 us  [expert_part(): lax.all_to_all(buffer_gate, 'ctx', split_axis=0, concat_axis=0, tiled=True)]
    all_to_all x1 -> x0, starting transfers between devices: 6.36 us -> none  [expert_part(): lax.all_to_all(buffer_cot, 'ctx', split_axis=0, concat_axis=0, tiled=True)]
  transfers between devices with their start and end apart: 7 -> 21, of which waited for: 4 -> 11; matrix products, arithmetic and copies ran while one was open for 8% -> 8% of each run, Pallas kernels for 0% -> 0%
where the time goes in v1:
time: 468 us; the launch traced here: 467 us
  waiting for transfers between devices  174 us (37%)
  blocking collectives  140 us (30%)
  starting transfers between devices  52.4 us (11%)
  matrix products  44.7 us (10%)
  other arithmetic  26.2 us (6%)
  between operations  16.8 us (4%)
  local copies, waits for them, and re-layouts  12.1 us (3%)
    unnamed x1, blocking collectives  116 us
    all_gather x2, waiting for transfers between devices, prefix(): lax.all_gather(a.astype(kind), axis)  93.8 us
    ppermute x15, waiting for transfers between devices, expert_part(): part = lax.ppermute(part, 'ctx', [(d, d ^ mask) for d in range(ways)])  66.1 us
    ppermute x15, starting transfers between devices, expert_part(): part = lax.ppermute(part, 'ctx', [(d, d ^ mask) for d in range(ways)])  33 us
    all_to_all x1, blocking collectives, expert_part(): lax.all_to_all(buffer_gate, 'ctx', split_axis=0, concat_axis=0, tiled=True)  23.8 us
    add x15, other arithmetic, chain_step(): jnp.exp(later[0])[:, None, None] * earlier[1] + later[1]  19.5 us
    psum x1, waiting for transfers between devices, expert_part(): lax.psum(part_back.astype(jnp.bfloat16), 'exp').astype(jnp.float32)  14.5 us
    dot_general x1, matrix products, expert_part(): lax.dot_general(slope_rows, up_local, (((1,), (1,)), ((), ())), preferred...  10.5 us
  transfers between devices with their start and end apart: 21, of which 11 were waited for; matrix products, arithmetic and copies ran while one was open for 8% of the time, Pallas kernels for 0%

profile of v1, /device:TPU:31, one launch (start us, length us, event | category | flops | bytes accessed | tf_op | source)
XLA Modules:
  0.0 466.9 jit_solution(11304046652859493189)
XLA Ops:
  14.0 6.5 %all-to-all-start.1 = ((bf16[16,40,2048]{2,1,0:T(8,128)(2,1)}), bf16[16,40,2048]{2,1,0:T(8,128)(2,1)}, u32[]{:S(2)}, u32[]{:S(2)}) async-start(bf16[16,40,2048]{2,1,0:T(8,128)(2,1)} %bitcast.25), calls=%async_computation.1 | async-start | bytes 5242880 | tf_op jit(solution)/shard_map/all_to_all | solution.py:133
  26.4 11.0 %collective-permute-done = bf16[1,40,2048]{2,1,0:T(8,128)(2,1)S(1)} collective-permute-done((bf16[1,40,2048]{2,1,0:T(8,128)(2,1)S(1)}, bf16[1,40,2048]{2,1,0:T(8,128)(2,1)S(1)}, u32[]{:S(2)}, u32[]{:S(2)}) %collective-permute-start) | collective-permute-done | bytes 163872 | tf_op jit(solution)/shard_map/ppermute | solution.py:144
  37.4 7.7 %collective-permute-done.1 = bf16[1,40,2048]{2,1,0:T(8,128)(2,1)S(1)} collective-permute-done((bf16[1,40,2048]{2,1,0:T(8,128)(2,1)S(1)}, bf16[1,40,2048]{2,1,0:T(8,128)(2,1)S(1)}, u32[]{:S(2)}, u32[]{:S(2)}) %collective-permute-start.1) | collective-permute-done | bytes 163872 | tf_op jit(solution)/shard_map/ppermute | solution.py:144
  45.1 4.0 collective-permute-start.7
  49.1 17.2 %collective-permute-done.3 = bf16[1,40,2048]{2,1,0:T(8,128)(2,1)S(1)} collective-permute-done((bf16[1,40,2048]{2,1,0:T(8,128)(2,1)S(1)}, bf16[1,40,2048]{2,1,0:T(8,128)(2,1)S(1)}, u32[]{:S(2)}, u32[]{:S(2)}) %collective-permute-start.3) | collective-permute-done | bytes 163872 | tf_op jit(solution)/shard_map/ppermute | solution.py:144
  66.9 3.0 collective-permute-done.4
  76.9 4.4 collective-permute-start.11
  81.3 17.7 %collective-permute-done.7 = bf16[1,40,2048]{2,1,0:T(8,128)(2,1)S(1)} collective-permute-done((bf16[1,40,2048]{2,1,0:T(8,128)(2,1)S(1)}, bf16[1,40,2048]{2,1,0:T(8,128)(2,1)S(1)}, u32[]{:S(2)}, u32[]{:S(2)}) %collective-permute-start.7) | collective-permute-done | bytes 163872 | tf_op jit(solution)/shard_map/ppermute | solution.py:144
  99.0 6.6 %collective-permute-start.12 = (bf16[1,40,2048]{2,1,0:T(8,128)(2,1)S(1)}, bf16[1,40,2048]{2,1,0:T(8,128)(2,1)S(1)}, u32[]{:S(2)}, u32[]{:S(2)}) collective-permute-start(bf16[1,40,2048]{2,1,0:T(8,128)(2,1)S(1)} %get-tuple-element.184), channel_id=1, source_target_pairs={{0,26},{2,24},{4,30},{6,28},{8,18},{10,16},{12,22},{14,20},{16,10}... | collective-permute-start | bytes 491528 | tf_op jit(solution)/shard_map/ppermute | solution.py:144
  105.8 2.7 collective-permute-done.9
  108.6 10.2 %collective-permute-start.14 = (bf16[1,40,2048]{2,1,0:T(8,128)(2,1)S(1)}, bf16[1,40,2048]{2,1,0:T(8,128)(2,1)S(1)}, u32[]{:S(2)}, u32[]{:S(2)}) collective-permute-start(bf16[1,40,2048]{2,1,0:T(8,128)(2,1)S(1)} %get-tuple-element.182), channel_id=1, source_target_pairs={{0,30},{2,28},{4,26},{6,24},{8,22},{10,20},{12,18},{14,16},{16,14}... | collective-permute-start | bytes 491528 | tf_op jit(solution)/shard_map/ppermute | solution.py:144
  118.9 2.6 collective-permute-done.14
  121.6 5.6 %fusion.14 = bf16[640,1536]{1,0:T(8,128)(2,1)} fusion(bf16[640,2048]{1,0:T(8,128)(2,1)S(1)} %bitcast.161, bf16[1,1536,2048]{2,1,0:T(8,128)(2,1)S(1)} %bitcast.169), kind=kOutput, calls=%fused_computation.23 | convolution fusion | flops 4027514880 | bytes 10878976 | tf_op jit(solution)/shard_map/dot_general | solution.py:153
  127.2 9.1 %fusion.17 = bf16[640,1536]{1,0:T(8,128)(2,1)} fusion(bf16[640,2048]{1,0:T(8,128)(2,1)} %bitcast.26, bf16[1,2048,1536]{2,1,0:T(8,128)(2,1)} %param.22), kind=kOutput, calls=%fused_computation.24 | convolution fusion | flops 4027514880 | bytes 10878976 | tf_op jit(solution)/shard_map/dot_general | solution.py:152
  141.4 23.8 %all_to_all.26 = bf16[16,1,40]{2,1,0:T(2,128)(2,1)S(1)} all-to-all(bf16[16,1,40]{2,1,0:T(2,128)(2,1)S(1)} %all_to_all.21), channel_id=1, replica_groups=mesh['ctx'=16,'exp'=2] {'ctx'}, dimensions={0} | all-to-all | bytes 2560 | tf_op jit(solution)/shard_map/all_to_all | solution.py:147
  165.4 14.5 %all-reduce.4.cloned.1.call-done = (bf16[640,1536]{1,0:T(8,128)(2,1)}, bf16[640,1536]{1,0:T(8,128)(2,1)}) async-done(((bf16[640,1536]{1,0:T(8,128)(2,1)}, bf16[640,1536]{1,0:T(8,128)(2,1)}), (bf16[640,1536]{1,0:T(8,128)(2,1)}, bf16[640,1536]{1,0:T(8,128)(2,1)})) %all-reduce.4.cloned.1.call-update) | async-done | bytes 3932176 | tf_op jit(solution)/shard_map/psum | solution.py:157
  179.8 3.4 fusion.8
  183.9 6.4 %all-to-all-start.3 = ((bf16[16,1,40]{2,1,0:T(2,128)(2,1)}), bf16[16,1,40]{2,1,0:T(2,128)(2,1)S(1)}, u32[]{:S(2)}, u32[]{:S(2)}) async-start(bf16[16,1,40]{2,1,0:T(2,128)(2,1)} %convert_element_type.212), calls=%async_computation.3 | async-start | bytes 16384 | tf_op jit(solution)/shard_map/all_to_all | solution.py:166
  190.3 10.5 %fusion.20 = bf16[640,2048]{1,0:T(8,128)(2,1)} fusion(bf16[1,2048,1536]{2,1,0:T(8,128)(2,1)} %param.22, bf16[640,1536]{1,0:T(8,128)(2,1)} %get-tuple-element.180, bf16[640,1536]{1,0:T(8,128)(2,1)} %get-tuple-element.181, f32[640]{0:T(1024)S(1)} %reshape.161), kind=kOutput, calls=%fused_computation.25 | convolution fusion | flops 4039639040 | bytes 12847616 | tf_op jit(solution)/shard_map/dot_general | solution.py:160
  200.8 6.5 %all-to-all-start.2 = ((bf16[16,40,2048]{2,1,0:T(8,128)(2,1)}), bf16[16,40,2048]{2,1,0:T(8,128)(2,1)S(1)}, u32[]{:S(2)}, u32[]{:S(2)}) async-start(bf16[16,40,2048]{2,1,0:T(8,128)(2,1)} %bitcast.160), calls=%async_computation.2 | async-start | bytes 5242880 | tf_op jit(solution)/shard_map/all_to_all | solution.py:165
  209.0 115.9 %all-reduce = bf16[256]{0:T(256)(128)(2,1)S(1)} all-reduce(bf16[256]{0:T(256)(128)(2,1)S(1)} %dynamic-update-slice), channel_id=2, replica_groups=mesh['ctx'=16,'exp'=2] {'ctx'}, use_global_device_ids=true, to_apply=%add | all-reduce | flops 256 | bytes 1024
  335.3 93.8 %all-gather.6.cloned.1.call-done = bf16[256,128,128]{2,1,0:T(8,128)(2,1)} async-done(((bf16[16,128,128]{2,1,0:T(8,128)(2,1)}), bf16[256,128,128]{2,1,0:T(8,128)(2,1)}) %all-gather.6.cloned.1.call-update) | async-done | bytes 8388624 | tf_op jit(solution)/shard_map/all_gather | solution.py:12
  429.3 20.2 %while.26 = (s32[]{:T(128)}, f32[16,128,128]{2,1,0:T(8,128)S(1)}, s32[]{:T(128)}, bf16[16,16]{1,0:T(8,128)(2,1)S(1)}, bf16[16,16,128,128]{3,2,1,0:T(8,128)(2,1)}, /*index=5*/s32[]{:T(128)}, s32[]{:T(128)}, s32[]{:T(128)}) while((s32[]{:T(128)}, f32[16,128,128]{2,1,0:T(8,128)S(1)}, s32[]{:T(128)}, bf16[16,16]{1,0:T(8,128)(2,1)S(1)}, ...), condition=%wide.region_2.3_spmd, body=%wide.region_1.2_spmd.sunk | while | flops 786453 | bytes 2621735 | solution.py:27
  449.5 2.4 fusion.40
  (164 shorter events, 64.2 us)
Async XLA Ops:
  14.0 113.2 %all-to-all-start.1 = ((bf16[16,40,2048]{2,1,0:T(8,128)(2,1)}), bf16[16,40,2048]{2,1,0:T(8,128)(2,1)}, u32[]{:S(2)}, u32[]{:S(2)}) async-start(bf16[16,40,2048]{2,1,0:T(8,128)(2,1)} %bitcast.25), calls=%async_computation.1 | async-start | bytes 5242880 | tf_op jit(solution)/shard_map/all_to_all | solution.py:133
  20.5 159.3 %all-reduce.4.cloned.1.call-start = ((), (), s32[]{:S(2)}) async-start(), calls=%async_computation.6 | async-start | bytes 7864320 | tf_op jit(solution)/shard_map/psum | solution.py:157
  21.5 100.0 %slice-start = ((s8[6291456]{0:T(1024)(128)(4,1)}), s8[4194304]{0:T(1024)(128)(4,1)S(1)}, s32[]{:S(2)}) async-start(s8[6291456]{0:T(1024)(128)(4,1)} %bitcast.168), calls=%async_computation.7 | async-start | bytes 8388608
  21.9 99.7 %slice-start.1 = ((s8[6291456]{0:T(1024)(128)(4,1)}), s8[2097152]{0:T(1024)(128)(4,1)S(1)}, s32[]{:S(2)}) async-start(s8[6291456]{0:T(1024)(128)(4,1)} %bitcast.168), calls=%async_computation.8 | async-start | bytes 4194304
  22.2 15.2 %collective-permute-start = (bf16[1,40,2048]{2,1,0:T(8,128)(2,1)S(1)}, bf16[1,40,2048]{2,1,0:T(8,128)(2,1)S(1)}, u32[]{:S(2)}, u32[]{:S(2)}) collective-permute-start(bf16[1,40,2048]{2,1,0:T(8,128)(2,1)S(1)} %get-tuple-element.196), channel_id=1, source_target_pairs={{0,2},{2,0},{4,6},{6,4},{8,10},{10,8},{12,14},{14,12},{16,18},{18,... | collective-permute-start | bytes 491528 | tf_op jit(solution)/shard_map/ppermute | solution.py:144
  22.5 22.6 %collective-permute-start.1 = (bf16[1,40,2048]{2,1,0:T(8,128)(2,1)S(1)}, bf16[1,40,2048]{2,1,0:T(8,128)(2,1)S(1)}, u32[]{:S(2)}, u32[]{:S(2)}) collective-permute-start(bf16[1,40,2048]{2,1,0:T(8,128)(2,1)S(1)} %get-tuple-element.195), channel_id=1, source_target_pairs={{0,4},{2,6},{4,0},{6,2},{8,12},{10,14},{12,8},{14,10},{16,20},{18,... | collective-permute-start | bytes 491528 | tf_op jit(solution)/shard_map/ppermute | solution.py:144
  22.8 22.3 %collective-permute-start.2 = (bf16[1,40,2048]{2,1,0:T(8,128)(2,1)S(1)}, bf16[1,40,2048]{2,1,0:T(8,128)(2,1)S(1)}, u32[]{:S(2)}, u32[]{:S(2)}) collective-permute-start(bf16[1,40,2048]{2,1,0:T(8,128)(2,1)S(1)} %get-tuple-element.194), channel_id=1, source_target_pairs={{0,6},{2,4},{4,2},{6,0},{8,14},{10,12},{12,10},{14,8},{16,22},{18,... | collective-permute-start | bytes 491528 | tf_op jit(solution)/shard_map/ppermute | solution.py:144
  24.9 41.5 %collective-permute-start.3 = (bf16[1,40,2048]{2,1,0:T(8,128)(2,1)S(1)}, bf16[1,40,2048]{2,1,0:T(8,128)(2,1)S(1)}, u32[]{:S(2)}, u32[]{:S(2)}) collective-permute-start(bf16[1,40,2048]{2,1,0:T(8,128)(2,1)S(1)} %get-tuple-element.193), channel_id=1, source_target_pairs={{0,8},{2,10},{4,12},{6,14},{8,0},{10,2},{12,4},{14,6},{16,24},{18,... | collective-permute-start | bytes 491528 | tf_op jit(solution)/shard_map/ppermute | solution.py:144
  25.2 44.7 %collective-permute-start.4 = (bf16[1,40,2048]{2,1,0:T(8,128)(2,1)S(1)}, bf16[1,40,2048]{2,1,0:T(8,128)(2,1)S(1)}, u32[]{:S(2)}, u32[]{:S(2)}) collective-permute-start(bf16[1,40,2048]{2,1,0:T(8,128)(2,1)S(1)} %get-tuple-element.192), channel_id=1, source_target_pairs={{0,10},{2,8},{4,14},{6,12},{8,2},{10,0},{12,6},{14,4},{16,26},{18,... | collective-permute-start | bytes 491528 | tf_op jit(solution)/shard_map/ppermute | solution.py:144
  37.4 36.0 %collective-permute-start.5 = (bf16[1,40,2048]{2,1,0:T(8,128)(2,1)S(1)}, bf16[1,40,2048]{2,1,0:T(8,128)(2,1)S(1)}, u32[]{:S(2)}, u32[]{:S(2)}) collective-permute-start(bf16[1,40,2048]{2,1,0:T(8,128)(2,1)S(1)} %get-tuple-element.191), channel_id=1, source_target_pairs={{0,12},{2,14},{4,8},{6,10},{8,4},{10,6},{12,0},{14,2},{16,28},{18,... | collective-permute-start | bytes 491528 | tf_op jit(solution)/shard_map/ppermute | solution.py:144
  45.1 31.8 %collective-permute-start.6 = (bf16[1,40,2048]{2,1,0:T(8,128)(2,1)S(1)}, bf16[1,40,2048]{2,1,0:T(8,128)(2,1)S(1)}, u32[]{:S(2)}, u32[]{:S(2)}) collective-permute-start(bf16[1,40,2048]{2,1,0:T(8,128)(2,1)S(1)} %get-tuple-element.190), channel_id=1, source_target_pairs={{0,14},{2,12},{4,10},{6,8},{8,6},{10,4},{12,2},{14,0},{16,30},{18,... | collective-permute-start | bytes 491528 | tf_op jit(solution)/shard_map/ppermute | solution.py:144
  45.1 53.8 %collective-permute-start.7 = (bf16[1,40,2048]{2,1,0:T(8,128)(2,1)S(1)}, bf16[1,40,2048]{2,1,0:T(8,128)(2,1)S(1)}, u32[]{:S(2)}, u32[]{:S(2)}) collective-permute-start(bf16[1,40,2048]{2,1,0:T(8,128)(2,1)S(1)} %get-tuple-element.189), channel_id=1, source_target_pairs={{0,16},{2,18},{4,20},{6,22},{8,24},{10,26},{12,28},{14,30},{16,0},... | collective-permute-start | bytes 491528 | tf_op jit(solution)/shard_map/ppermute | solution.py:144
  66.4 39.2 %collective-permute-start.8 = (bf16[1,40,2048]{2,1,0:T(8,128)(2,1)S(1)}, bf16[1,40,2048]{2,1,0:T(8,128)(2,1)S(1)}, u32[]{:S(2)}, u32[]{:S(2)}) collective-permute-start(bf16[1,40,2048]{2,1,0:T(8,128)(2,1)S(1)} %get-tuple-element.188), channel_id=1, source_target_pairs={{0,18},{2,16},{4,22},{6,20},{8,26},{10,24},{12,30},{14,28},{16,2},... | collective-permute-start | bytes 491528 | tf_op jit(solution)/shard_map/ppermute | solution.py:144
  69.9 38.7 %collective-permute-start.9 = (bf16[1,40,2048]{2,1,0:T(8,128)(2,1)S(1)}, bf16[1,40,2048]{2,1,0:T(8,128)(2,1)S(1)}, u32[]{:S(2)}, u32[]{:S(2)}) collective-permute-start(bf16[1,40,2048]{2,1,0:T(8,128)(2,1)S(1)} %get-tuple-element.187), channel_id=1, source_target_pairs={{0,20},{2,22},{4,16},{6,18},{8,28},{10,30},{12,24},{14,26},{16,4},... | collective-permute-start | bytes 491528 | tf_op jit(solution)/shard_map/ppermute | solution.py:144
  73.4 45.4 %collective-permute-start.10 = (bf16[1,40,2048]{2,1,0:T(8,128)(2,1)S(1)}, bf16[1,40,2048]{2,1,0:T(8,128)(2,1)S(1)}, u32[]{:S(2)}, u32[]{:S(2)}) collective-permute-start(bf16[1,40,2048]{2,1,0:T(8,128)(2,1)S(1)} %get-tuple-element.186), channel_id=1, source_target_pairs={{0,22},{2,20},{4,18},{6,16},{8,30},{10,28},{12,26},{14,24},{16,6},... | collective-permute-start | bytes 491528 | tf_op jit(solution)/shard_map/ppermute | solution.py:144
  76.9 41.9 %collective-permute-start.11 = (bf16[1,40,2048]{2,1,0:T(8,128)(2,1)S(1)}, bf16[1,40,2048]{2,1,0:T(8,128)(2,1)S(1)}, u32[]{:S(2)}, u32[]{:S(2)}) collective-permute-start(bf16[1,40,2048]{2,1,0:T(8,128)(2,1)S(1)} %get-tuple-element.185), channel_id=1, source_target_pairs={{0,24},{2,26},{4,28},{6,30},{8,16},{10,18},{12,20},{14,22},{16,8},... | collective-permute-start | bytes 491528 | tf_op jit(solution)/shard_map/ppermute | solution.py:144
  99.0 19.8 %collective-permute-start.12 = (bf16[1,40,2048]{2,1,0:T(8,128)(2,1)S(1)}, bf16[1,40,2048]{2,1,0:T(8,128)(2,1)S(1)}, u32[]{:S(2)}, u32[]{:S(2)}) collective-permute-start(bf16[1,40,2048]{2,1,0:T(8,128)(2,1)S(1)} %get-tuple-element.184), channel_id=1, source_target_pairs={{0,26},{2,24},{4,30},{6,28},{8,18},{10,16},{12,22},{14,20},{16,10}... | collective-permute-start | bytes 491528 | tf_op jit(solution)/shard_map/ppermute | solution.py:144
  105.6 13.3 %collective-permute-start.13 = (bf16[1,40,2048]{2,1,0:T(8,128)(2,1)S(1)}, bf16[1,40,2048]{2,1,0:T(8,128)(2,1)S(1)}, u32[]{:S(2)}, u32[]{:S(2)}) collective-permute-start(bf16[1,40,2048]{2,1,0:T(8,128)(2,1)S(1)} %get-tuple-element.183), channel_id=1, source_target_pairs={{0,28},{2,30},{4,24},{6,26},{8,20},{10,22},{12,16},{14,18},{16,12}... | collective-permute-start | bytes 491528 | tf_op jit(solution)/shard_map/ppermute | solution.py:144
  108.6 13.0 %collective-permute-start.14 = (bf16[1,40,2048]{2,1,0:T(8,128)(2,1)S(1)}, bf16[1,40,2048]{2,1,0:T(8,128)(2,1)S(1)}, u32[]{:S(2)}, u32[]{:S(2)}) collective-permute-start(bf16[1,40,2048]{2,1,0:T(8,128)(2,1)S(1)} %get-tuple-element.182), channel_id=1, source_target_pairs={{0,30},{2,28},{4,26},{6,24},{8,22},{10,20},{12,18},{14,16},{16,14}... | collective-permute-start | bytes 491528 | tf_op jit(solution)/shard_map/ppermute | solution.py:144
  136.4 194.9 %all-gather.8.cloned.1.call-start = ((), (), s32[]{:S(2)}) async-start(), calls=%async_computation.5 | async-start | bytes 8912896 | tf_op jit(solution)/shard_map/all_gather | solution.py:12
  137.3 63.4 %copy-start.4 = (bf16[128,2048]{0,1:T(8,128)(2,1)}, bf16[128,2048]{0,1:T(8,128)(2,1)S(1)}, u32[]{:S(2)}) copy-start(bf16[128,2048]{0,1:T(8,128)(2,1)S(1)} %copy.124) | copy-start | bytes 1572868
  139.5 289.7 %all-gather.6.cloned.1.call-start = ((), (), s32[]{:S(2)}) async-start(), calls=%async_computation.4 | async-start | bytes 8912896 | tf_op jit(solution)/shard_map/all_gather | solution.py:12
  183.9 16.9 %all-to-all-start.3 = ((bf16[16,1,40]{2,1,0:T(2,128)(2,1)}), bf16[16,1,40]{2,1,0:T(2,128)(2,1)S(1)}, u32[]{:S(2)}, u32[]{:S(2)}) async-start(bf16[16,1,40]{2,1,0:T(2,128)(2,1)} %convert_element_type.212), calls=%async_computation.3 | async-start | bytes 16384 | tf_op jit(solution)/shard_map/all_to_all | solution.py:166
  200.8 129.1 %all-to-all-start.2 = ((bf16[16,40,2048]{2,1,0:T(8,128)(2,1)}), bf16[16,40,2048]{2,1,0:T(8,128)(2,1)S(1)}, u32[]{:S(2)}, u32[]{:S(2)}) async-start(bf16[16,40,2048]{2,1,0:T(8,128)(2,1)} %bitcast.160), calls=%async_computation.2 | async-start | bytes 5242880 | tf_op jit(solution)/shard_map/all_to_all | solution.py:165
  (15 other events, 66.9 us)
Sparse Core Ops, SparseCore 0:
  136.5 43.3 all-reduce.3
Sparse Core Ops, SparseCore 1:
  140.2 174.8 all-gather.7
  318.3 110.8 all-gather.5
